TPU v7x, 128 devices: a whole 4x4x4 slice. The times are simulated.
128 devices in a mesh: req: 16 (over z, y), kv: 8 (over x, core).
Axes of the slice: x: 4, y: 4, z: 4, core: 2. Of those that a mesh axis runs over, the one named last changes fastest.
Arguments:
- hidden_in: bfloat16 [16384, 2048], P(('req', 'kv')), may hold values from -6 to 6
- slot_tokens: int32 [16384], replicated, may hold values from 0 to 16383, as said below
- cache_len: int32 [128], P('req'), may hold values from 1 to 2048, 65536 in all
- prefill_start: int32 [16], P('req'), may hold values from 0 to 2048
- key_cache: bfloat16 [128, 2048, 1024], P('req', None, 'kv')
- value_cache: bfloat16 [128, 2048, 1024], P('req', None, 'kv'), may hold values from -18 to 18
- key_prefix: bfloat16 [16, 2048, 1024], P('req', None, 'kv')
- value_prefix: bfloat16 [16, 2048, 1024], P('req', None, 'kv'), may hold values from -18 to 18
- attn_gain: float32 [2048], replicated, may hold values from 0.25 to 1.75
- q_proj: bfloat16 [2048, 2048], P(None, 'kv'), may hold values from -0.125 to 0.125
- k_proj: bfloat16 [2048, 1024], P(None, 'kv'), may hold values from -0.125 to 0.125
- v_proj: bfloat16 [2048, 1024], P(None, 'kv'), may hold values from -0.125 to 0.125
- q_gain: float32 [128], replicated, may hold values from 0.25 to 1.75
- k_gain: float32 [128], replicated, may hold values from 0.25 to 1.75
- o_proj: bfloat16 [2048, 2048], P('kv'), may hold values from -0.125 to 0.125
- ffn_gain: float32 [2048], replicated, may hold values from 0.25 to 1.75
- w_gate: bfloat16 [2048, 6144], P(None, 'req'), may hold values from -0.125 to 0.125
- w_up: bfloat16 [2048, 6144], P(None, 'req'), may hold values from -0.125 to 0.125
- w_down: bfloat16 [6144, 2048], P('req'), may hold values from -0.078125 to 0.078125
- final_gain: float32 [2048], replicated, may hold values from 0.25 to 1.75
- lm_head: bfloat16 [2048, 151936], P(None, ('req', 'kv')), may hold values from -0.375 to 0.375
Outputs:
- layer_out: bfloat16 [16384, 2048], P(('req', 'kv'))
- max_logit: float32 [144], replicated
Inputs may be any that keep to these rules, and one draw needn't show every extreme that they name: slot_tokens is a permutation of the batch's tokens; each device's 128 consecutive slots take exactly 1 token from each device's 128 consecutive batch tokens.
All inputs are finite; a program needn't handle non-finite values. No bound on the sum of `cache_len` on one device may be relied on, other than what follows from the above.
Results may differ from a plain program's by a relative error of at most 0.0085.
The roundings to bfloat16 on the way count: a program that leaves them out, or rounds other values in their place, can miss the bound.
Values may be sent and summed in bfloat16 or wider, within the bound.
A program may use at most 128 MiB of HBM per device.

v0:
```python
import jax
import jax.numpy as jnp
from jax import lax
from jax.sharding import PartitionSpec as P

EPS = 1e-06
NEG = -1e30


def spread(value, axis, root):
    mine = lax.axis_index(axis) == root
    return lax.psum(jnp.where(mine, value, jnp.zeros_like(value)), axis)


def norm_rows(values, gain_vec):
    wide = values.astype(jnp.float32)
    return wide * lax.rsqrt(jnp.mean(wide * wide, axis=-1, keepdims=True) + EPS) * gain_vec


def rotate(values, places):
    half_dim = values.shape[-1] // 2
    freqs = 1000000.0 ** (-(jnp.arange(half_dim, dtype=jnp.float32) * 2.0 / values.shape[-1]))
    angles = places[:, None] * freqs[None, :]
    cosine = jnp.cos(angles)[:, None, :]
    sine = jnp.sin(angles)[:, None, :]
    first_half = values[..., :half_dim]
    second_half = values[..., half_dim:]
    return jnp.concatenate(
        [first_half * cosine - second_half * sine, second_half * cosine + first_half * sine],
        axis=-1,
    )


def prefill_full(q_heads, key_old, value_old, key_new, value_new, start_at):
    old_len = key_old.shape[0]
    fresh_rows = q_heads.shape[0]
    factor = q_heads.shape[-1] ** (-0.5)
    all_keys = jnp.concatenate([key_old, key_new], axis=0)
    all_values = jnp.concatenate([value_old, value_new], axis=0)
    scores = (
        jnp.einsum("cgd,kd->gck", q_heads, all_keys, preferred_element_type=jnp.float32) * factor
    )
    key_index = jnp.arange(old_len + fresh_rows, dtype=jnp.int32)[None, :]
    row_index = jnp.arange(fresh_rows, dtype=jnp.int32)[:, None]
    allowed = jnp.where(key_index < old_len, key_index < start_at, key_index - old_len <= row_index)
    scores = jnp.where(allowed[None], scores, NEG)
    row_peak = jnp.max(scores, axis=-1, keepdims=True)
    expd = jnp.exp(scores - row_peak)
    weights = (expd / jnp.sum(expd, axis=-1, keepdims=True)).astype(jnp.bfloat16)
    return jnp.einsum(
        "gck,kd->cgd", weights, all_values, preferred_element_type=jnp.float32
    ).astype(jnp.bfloat16)


def decode_attend(q_heads, key_old, value_old, key_self, value_self, lengths):
    factor = q_heads.shape[-1] ** (-0.5)
    past = jnp.einsum("bgd,bld->bgl", q_heads, key_old, preferred_element_type=jnp.float32) * factor
    slot_index = jnp.arange(key_old.shape[1], dtype=jnp.int32)
    past = jnp.where(slot_index[None, None, :] < lengths[:, None, None], past, NEG)
    own_score = (
        jnp.einsum("bgd,bd->bg", q_heads, key_self, preferred_element_type=jnp.float32) * factor
    )
    row_peak = jnp.maximum(jnp.max(past, axis=-1), own_score)
    past_exp = jnp.exp(past - row_peak[..., None])
    own_exp = jnp.exp(own_score - row_peak)
    row_total = jnp.sum(past_exp, axis=-1) + own_exp
    past_w = (past_exp / row_total[..., None]).astype(jnp.bfloat16)
    own_w = (own_exp / row_total).astype(jnp.bfloat16)
    summed = jnp.einsum("bgl,bld->bgd", past_w, value_old, preferred_element_type=jnp.float32)
    summed = (
        summed + own_w.astype(jnp.float32)[..., None] * value_self.astype(jnp.float32)[:, None, :]
    )
    return summed.astype(jnp.bfloat16)


def regroup(rows_in):
    return lax.all_to_all(rows_in, ("req", "kv"), split_axis=0, concat_axis=0, tiled=True)


def shards(
    hidden_in,
    slot_tokens,
    cache_len,
    prefill_start,
    key_cache,
    value_cache,
    key_prefix,
    value_prefix,
    attn_gain,
    q_proj,
    k_proj,
    v_proj,
    q_gain,
    k_gain,
    o_proj,
    ffn_gain,
    w_gate,
    w_up,
    w_down,
    final_gain,
    lm_head,
):
    req_count = lax.axis_size("req")
    kv_count = lax.axis_size("kv")
    devices = req_count * kv_count
    rows_dev = hidden_in.shape[0]
    kv_index = lax.axis_index("kv")
    self_index = lax.axis_index("req") * kv_count + kv_index
    slot_table = slot_tokens.reshape(devices, rows_dev)
    from_self = slot_table // rows_dev == self_index
    send_rows = jnp.sum(jnp.where(from_self, slot_table - self_index * rows_dev, 0), axis=1)
    slot_place = lax.dynamic_index_in_dim(slot_table, self_index, 0, keepdims=False) // rows_dev
    arrived = regroup(hidden_in[send_rows])
    owner_rows = arrived[slot_place]
    rows_all = lax.all_gather(owner_rows, "kv", axis=0, tiled=True)
    normed = norm_rows(rows_all, attn_gain).astype(jnp.bfloat16)
    o_full = lax.all_gather(o_proj, "kv", axis=0, tiled=True)
    ff_dev = w_gate.shape[1]
    ff_piece = ff_dev // kv_count
    gate_w = lax.all_gather(
        lax.dynamic_slice_in_dim(w_gate, kv_index * ff_piece, ff_piece, axis=1),
        "req",
        axis=1,
        tiled=True,
    )
    up_w = lax.all_gather(
        lax.dynamic_slice_in_dim(w_up, kv_index * ff_piece, ff_piece, axis=1),
        "req",
        axis=1,
        tiled=True,
    )
    down_w = lax.all_gather(
        lax.dynamic_slice_in_dim(w_down, kv_index * ff_piece, ff_piece, axis=0),
        "req",
        axis=0,
        tiled=True,
    )
    q_cols = q_proj.shape[1]
    kv_cols = k_proj.shape[1]
    projected = jnp.concatenate(
        [
            jnp.dot(normed, q_proj, preferred_element_type=jnp.float32),
            jnp.dot(normed, k_proj, preferred_element_type=jnp.float32),
            jnp.dot(normed, v_proj, preferred_element_type=jnp.float32),
        ],
        axis=1,
    )
    tok_req = projected.shape[0]
    head_dim = q_gain.shape[0]
    dec_count = cache_len.shape[0]
    fresh_count = tok_req - dec_count
    q_raw = projected[:, :q_cols].reshape(tok_req, q_cols // head_dim, head_dim)
    k_raw = projected[:, q_cols : q_cols + kv_cols].reshape(tok_req, kv_cols // head_dim, head_dim)
    v_new = (
        projected[:, q_cols + kv_cols :]
        .astype(jnp.bfloat16)
        .reshape(tok_req, kv_cols // head_dim, head_dim)
    )
    places = jnp.concatenate(
        [prefill_start[0] + jnp.arange(fresh_count, dtype=jnp.int32), cache_len]
    ).astype(jnp.float32)
    queries = rotate(norm_rows(q_raw, q_gain), places).astype(jnp.bfloat16)
    keys_new = rotate(norm_rows(k_raw, k_gain), places).astype(jnp.bfloat16)
    pre_out = prefill_full(
        queries[:fresh_count],
        key_prefix[0, :, 0:head_dim],
        value_prefix[0, :, 0:head_dim],
        keys_new[:fresh_count, 0],
        v_new[:fresh_count, 0],
        prefill_start[0],
    )
    dec_out = decode_attend(
        queries[fresh_count:],
        key_cache,
        value_cache,
        keys_new[fresh_count:, 0],
        v_new[fresh_count:, 0],
        cache_len,
    )
    pieces = jnp.concatenate([pre_out, dec_out], axis=0)
    pieces, gate_w, up_w, down_w = lax.optimization_barrier((pieces, gate_w, up_w, down_w))
    attended = lax.all_gather(pieces.reshape(tok_req, q_cols), "kv", axis=1, tiled=True)
    resid = (
        rows_all.astype(jnp.float32) + jnp.dot(attended, o_full, preferred_element_type=jnp.float32)
    ).astype(jnp.bfloat16)
    ffn_in = norm_rows(resid, ffn_gain).astype(jnp.bfloat16)
    gate_part = jnp.dot(ffn_in, gate_w, preferred_element_type=jnp.float32)
    up_part = jnp.dot(ffn_in, up_w, preferred_element_type=jnp.float32)
    hidden_act = (jax.nn.silu(gate_part) * up_part).astype(jnp.bfloat16)
    down_part = jnp.dot(hidden_act, down_w, preferred_element_type=jnp.float32)
    ffn_part = lax.psum_scatter(down_part, "kv", scatter_dimension=0, tiled=True)
    mine = lax.dynamic_slice_in_dim(resid, kv_index * rows_dev, rows_dev, axis=0)
    out_rows = (mine.astype(jnp.float32) + ffn_part).astype(jnp.bfloat16)
    going_back = jnp.zeros_like(out_rows).at[slot_place].set(out_rows)
    returned = regroup(going_back)
    layer_out = jnp.zeros_like(hidden_in).at[send_rows].set(returned)
    tail_sum = lax.psum(down_part[fresh_count - 1 :], "kv")
    tail_out = (resid[fresh_count - 1 :].astype(jnp.float32) + tail_sum).astype(jnp.bfloat16)
    tail_rows = norm_rows(tail_out, final_gain).astype(jnp.bfloat16)
    local_peaks = jnp.max(
        jnp.dot(
            lax.all_gather(tail_rows, "req", axis=0, tiled=True),
            lm_head,
            preferred_element_type=jnp.float32,
        ),
        axis=1,
    )
    max_logit = lax.pmax(local_peaks, ("req", "kv"))
    return (layer_out, max_logit)


def solution(mesh):
    placed = (
        P(("req", "kv"), None),
        P(),
        P("req"),
        P("req"),
        P("req", None, "kv"),
        P("req", None, "kv"),
        P("req", None, "kv"),
        P("req", None, "kv"),
        P(),
        P(None, "kv"),
        P(None, "kv"),
        P(None, "kv"),
        P(),
        P(),
        P("kv", None),
        P(),
        P(None, "req"),
        P(None, "req"),
        P("req", None),
        P(),
        P(None, ("req", "kv")),
    )
    return jax.shard_map(
        shards, mesh=mesh, in_specs=placed, out_specs=(P(("req", "kv"), None), P()), check_vma=False
    )
```

profile of v0, /device:TPU:1, one launch (start us, length us, event | category | flops | bytes accessed | tf_op | source)
XLA Modules:
  0.0 573.7 jit_solution(5138658079195809557)
XLA Ops:
  8.3 2.6 gather_fusion
  13.5 11.5 %all-to-all-start = ((bf16[128,2,1024]{2,1,0:T(2,128)(2,1)}), bf16[128,2,1024]{2,1,0:T(2,128)(2,1)S(1)}, u32[]{:S(2)}, u32[]{:S(2)}) async-start(bf16[128,2,1024]{2,1,0:T(2,128)(2,1)} %reshape.450), calls=%async_computation | async-start | bytes 1048576 | tf_op jit(solution)/shard_map/all_to_all | solution.py:77
  25.8 13.0 %all-to-all-done = bf16[128,2,1024]{2,1,0:T(2,128)(2,1)S(1)} async-done(((bf16[128,2,1024]{2,1,0:T(2,128)(2,1)}), bf16[128,2,1024]{2,1,0:T(2,128)(2,1)S(1)}, u32[]{:S(2)}, u32[]{:S(2)}) %all-to-all-start) | async-done | bytes 524320 | tf_op jit(solution)/shard_map/all_to_all | solution.py:77
  50.5 4.0 fusion.4
  54.5 15.7 %all-gather.19.cloned.1.call-done = bf16[1024,2048]{1,0:T(8,128)(2,1)} async-done(((bf16[128,2048]{1,0:T(8,128)(2,1)}), bf16[1024,2048]{1,0:T(8,128)(2,1)}) %all-gather.19.cloned.1.call-update) | async-done | bytes 4194320 | tf_op jit(solution)/shard_map/all_gather | solution.py:115
  70.1 3.2 fusion.10
  78.7 3.7 multiply_reduce_fusion.1
  88.2 3.6 convolution_convert_fusion
  92.6 15.9 %fusion.78 = (f32[2,1016]{1,0:T(2,128)S(1)}, f32[2,1016,3064]{2,1,0:T(8,128)}) fusion(pred[1016,3064]{1,0:T(8,128)(4,1)} %fusion.4, bf16[1016,128]{1,0:T(8,128)(2,1)S(1)} %copy.47, bf16[2048,128]{1,0:T(8,128)(2,1)S(1)} %bitcast.93, bf16[1024,2,64]{2,0,1:T(8,128)(2,1)S(1)} %get-tuple-element.10, bf16[1024,2,64]{2,0,1:T(8,128)(2,1)S(1)} %get-tuple-element.11), kind=kOutput, calls=%fused_computation.144 | convolution fusion | flops 1621384704 | bytes 29334016 | tf_op jit(solution)/shard_map/sub | solution.py:48
  108.5 12.0 %fusion.18 = bf16[1016,2,128]{2,0,1:T(8,128)(2,1)S(1)} fusion(f32[2,1016,3064]{2,1,0:T(8,128)} %get-tuple-element.25, f32[2,1016]{1,0:T(2,128)S(1)} %get-tuple-element.24, bf16[1016,128]{1,0:T(8,128)(2,1)S(1)} %slice.54, bf16[2048,128]{1,0:T(8,128)(2,1)S(1)} %bitcast.94), kind=kOutput, calls=%fused_computation.32 | convolution fusion | flops 1608149248 | bytes 26216896 | tf_op jit(solution)/shard_map/gck,kd->cgd/dot_general | solution.py:50
  120.6 48.2 %all-gather.11.cloned.1.call-done = bf16[2048,768]{0,1:T(8,128)(2,1)} async-done(((bf16[2048,48]{0,1:T(8,128)(2,1)}), bf16[2048,768]{0,1:T(8,128)(2,1)}) %all-gather.11.cloned.1.call-update) | async-done | bytes 3145744 | tf_op jit(solution)/shard_map/all_gather | solution.py:126
  168.8 48.9 %all-gather.13.cloned.1.call-done = bf16[768,2048]{1,0:T(8,128)(2,1)} async-done(((bf16[48,2048]{1,0:T(8,128)(2,1)}), bf16[768,2048]{1,0:T(8,128)(2,1)}) %all-gather.13.cloned.1.call-update) | async-done | bytes 3145744 | tf_op jit(solution)/shard_map/all_gather | solution.py:132
  218.8 49.7 %all-gather.17.cloned.1.call-done = bf16[2048,2048]{1,0:T(8,128)(2,1)} async-done(((bf16[256,2048]{1,0:T(8,128)(2,1)}), bf16[2048,2048]{1,0:T(8,128)(2,1)}) %all-gather.17.cloned.1.call-update) | async-done | bytes 8388624 | tf_op jit(solution)/shard_map/all_gather | solution.py:117
  268.5 34.4 %all-gather.15.cloned.1.call-done = bf16[1024,2048]{0,1:T(8,128)(2,1)} async-done(((bf16[1024,256]{0,1:T(8,128)(2,1)}), bf16[1024,2048]{0,1:T(8,128)(2,1)}) %all-gather.15.cloned.1.call-update) | async-done | bytes 4194320 | tf_op jit(solution)/shard_map/all_gather | solution.py:182
  302.9 14.2 %fusion.7 = (f32[1024]{0:T(1024)S(1)}, bf16[1024,2048]{1,0:T(8,128)(2,1)S(1)}) fusion(bf16[1024,2048]{0,1:T(8,128)(2,1)} %all-gather.15.cloned.1.call-done, bf16[2048,2048]{1,0:T(8,128)(2,1)} %all-gather.17.cloned.1.call-done, bf16[1024,2048]{1,0:T(8,128)(2,1)} %all-gather.19.cloned.1.call-done), kind=kOutput, calls=%fused_computation.20 | convolution fusion | flops 8602516480 | bytes 20975616 | tf_op jit(solution)/shard_map/dot_general | solution.py:184
  319.0 7.1 %fusion.20 = f32[1024,768]{1,0:T(8,128)} fusion(bf16[2048,768]{0,1:T(8,128)(2,1)} %all-gather.9.cloned.1.call-done, bf16[1024,2048]{1,0:T(8,128)(2,1)S(1)} %get-tuple-element.27, f32[2048]{0:T(1024)S(1)} %copy-done.17, f32[1024]{0:T(1024)S(1)} %add_rsqrt_fusion.1), kind=kOutput, calls=%fused_computation.33 | convolution fusion | flops 3229614080 | bytes 10498048 | tf_op jit(solution)/shard_map/dot_general | solution.py:187
  326.2 14.1 %fusion.23 = f32[1024,2048]{1,0:T(8,128)} fusion(bf16[768,2048]{1,0:T(8,128)(2,1)} %all-gather.13.cloned.1.call-done, f32[1024,768]{1,0:T(8,128)} %fusion.20, bf16[2048,768]{0,1:T(8,128)(2,1)} %all-gather.11.cloned.1.call-done, bf16[1024,2048]{1,0:T(8,128)(2,1)} %copy-done.7, f32[2048]{0:T(1024)S(1)} %copy-done.17, f32[1024]{0:T(1024)S(1)} %add_rsqrt_fusion.1), kind=kOutput, calls=%fused_computation.34 | convolution fusion | flops 6455558144 | bytes 22032384 | tf_op jit(solution)/shard_map/dot_general | solution.py:190
  342.6 56.0 %all-reduce.2.cloned.1.call-done = f32[9,2048]{1,0:T(8,128)} async-done(((f32[9,2048]{1,0:T(8,128)}), f32[9,2048]{1,0:T(8,128)}) %all-reduce.2.cloned.1.call-update) | async-done | bytes 73744 | tf_op jit(solution)/shard_map/psum | solution.py:197
  400.6 53.5 %reduce-scatter.2.cloned.1.call-done = f32[128,2048]{1,0:T(8,128)} async-done(((f32[1024,2048]{1,0:T(8,128)}), f32[128,2048]{1,0:T(8,128)}) %reduce-scatter.2.cloned.1.call-update) | async-done | bytes 1048592 | tf_op jit(solution)/shard_map/reduce_scatter | solution.py:191
  454.1 2.6 scatter_custom_fusion
  458.9 8.4 %all-to-all-start.1 = ((bf16[128,2,1024]{2,1,0:T(2,128)(2,1)}), bf16[128,2,1024]{2,1,0:T(2,128)(2,1)S(1)}, u32[]{:S(2)}, u32[]{:S(2)}) async-start(bf16[128,2,1024]{2,1,0:T(2,128)(2,1)} %reshape.452), calls=%async_computation.2 | async-start | bytes 1048576 | tf_op jit(solution)/shard_map/all_to_all | solution.py:77
  467.3 22.4 %all-gather.1 = bf16[16,9,2048]{2,1,0:T(8,128)(2,1)S(1)} all-gather(bf16[1,9,2048]{2,1,0:T(8,128)(2,1)S(1)} %fusion.51), channel_id=1, replica_groups=mesh['req'=16,'kv'=8] {'req'}, dimensions={0}, use_global_device_ids=true | all-gather | bytes 626688 | tf_op jit(solution)/shard_map/all_gather | solution.py:202
  490.8 4.4 convolution_reduce_fusion
  495.2 68.5 %pmax.7 = f32[144]{0:T(256)} all-reduce(f32[144]{0:T(256)S(1)} %convolution_reduce_fusion), channel_id=1, replica_groups=mesh['req'=16,'kv'=8] {'req','kv'}, use_global_device_ids=true, to_apply=%region_15.16 | all-reduce | flops 144 | bytes 1152 | tf_op jit(solution)/shard_map/pmax | solution.py:208
  (114 shorter events, 40.7 us)
Async XLA Ops:
  7.2 34.2 %copy-start = (bf16[2048,384]{1,0:T(8,128)(2,1)S(1)}, bf16[2048,384]{1,0:T(8,128)(2,1)}, u32[]{:S(2)}) copy-start(bf16[2048,384]{1,0:T(8,128)(2,1)} %param.37) | copy-start | bytes 4718596
  13.5 25.2 %all-to-all-start = ((bf16[128,2,1024]{2,1,0:T(2,128)(2,1)}), bf16[128,2,1024]{2,1,0:T(2,128)(2,1)S(1)}, u32[]{:S(2)}, u32[]{:S(2)}) async-start(bf16[128,2,1024]{2,1,0:T(2,128)(2,1)} %reshape.450), calls=%async_computation | async-start | bytes 1048576 | tf_op jit(solution)/shard_map/all_to_all | solution.py:77
  25.0 45.1 %all-gather.19.cloned.1.call-start = ((), (), s32[]{:S(2)}) async-start(), calls=%async_computation.10 | async-start | bytes 4718592 | tf_op jit(solution)/shard_map/all_gather | solution.py:115
  41.2 7.1 %copy-start.10 = (s32[8]{0:T(128)S(1)}, s32[8]{0:T(128)}, u32[]{:S(2)}) copy-start(s32[8]{0:T(128)} %param.23) | copy-start | bytes 100
  41.3 79.3 %all-gather.9.cloned.1.call-start = ((), (), s32[]{:S(2)}) async-start(), calls=%async_computation.3 | async-start | bytes 3342336 | tf_op jit(solution)/shard_map/all_gather | solution.py:120
  42.5 126.3 %all-gather.11.cloned.1.call-start = ((), (), s32[]{:S(2)}) async-start(), calls=%async_computation.4 | async-start | bytes 3342336 | tf_op jit(solution)/shard_map/all_gather | solution.py:126
  44.8 172.8 %all-gather.13.cloned.1.call-start = ((), (), s32[]{:S(2)}) async-start(), calls=%async_computation.5 | async-start | bytes 3342336 | tf_op jit(solution)/shard_map/all_gather | solution.py:132
  46.5 221.9 %all-gather.17.cloned.1.call-start = ((), (), s32[]{:S(2)}) async-start(), calls=%async_computation.7 | async-start | bytes 9437184 | tf_op jit(solution)/shard_map/all_gather | solution.py:117
  47.1 255.8 %all-gather.15.cloned.1.call-start = ((), (), s32[]{:S(2)}) async-start(), calls=%async_computation.6 | async-start | bytes 4718592 | tf_op jit(solution)/shard_map/all_gather | solution.py:182
  48.5 24.9 %copy-start.8 = (f32[2048]{0:T(1024)S(1)}, f32[2048]{0:T(1024)}, u32[]{:S(2)}) copy-start(f32[2048]{0:T(1024)} %param.29) | copy-start | bytes 24580
  70.1 3.4 copy-start.2
  74.8 3.9 copy-start.6
  77.1 5.3 copy-start.11
  78.7 5.4 copy-start.12
  84.9 3.2 copy-start.14
  88.1 3.7 copy-start.5
  88.2 4.5 copy-start.15
  92.6 15.9 %copy-start.16 = (bf16[1,2048,128]{2,1,0:T(8,128)(2,1)S(1)}, bf16[1,2048,128]{2,1,0:T(8,128)(2,1)}, u32[]{:S(2)}) copy-start(bf16[1,2048,128]{2,1,0:T(8,128)(2,1)} %param.28) | copy-start | bytes 1572868
  218.7 100.3 %copy-start.17 = (f32[2048]{0:T(1024)S(1)}, f32[2048]{0:T(1024)}, u32[]{:S(2)}) copy-start(f32[2048]{0:T(1024)} %param.36) | copy-start | bytes 24580
  218.7 179.8 %all-reduce.2.cloned.1.call-start = ((), (), s32[]{:S(2)}) async-start(), calls=%async_computation.9 | async-start | bytes 262144 | tf_op jit(solution)/shard_map/psum | solution.py:197
  341.8 57.8 %copy-start.9 = (f32[2048]{0:T(1024)S(1)}, f32[2048]{0:T(1024)}, u32[]{:S(2)}) copy-start(f32[2048]{0:T(1024)} %param.40) | copy-start | bytes 24580
  341.8 112.3 %reduce-scatter.2.cloned.1.call-start = ((), (), s32[]{:S(2)}) async-start(), calls=%async_computation.8 | async-start | bytes 9437184 | tf_op jit(solution)/shard_map/reduce_scatter | solution.py:191
  458.9 104.8 %all-to-all-start.1 = ((bf16[128,2,1024]{2,1,0:T(2,128)(2,1)}), bf16[128,2,1024]{2,1,0:T(2,128)(2,1)S(1)}, u32[]{:S(2)}, u32[]{:S(2)}) async-start(bf16[128,2,1024]{2,1,0:T(2,128)(2,1)} %reshape.452), calls=%async_computation.2 | async-start | bytes 1048576 | tf_op jit(solution)/shard_map/all_to_all | solution.py:77
  489.7 76.9 %copy-start.1 = (bf16[2048,384]{1,0:T(8,128)(2,1)S(1)}, bf16[2048,384]{1,0:T(8,128)(2,1)}, u32[]{:S(2)}) copy-start(bf16[2048,384]{1,0:T(8,128)(2,1)} %param.37) | copy-start | bytes 4718596
  (4 other events, 7.7 us)
Sparse Core Ops, SparseCore 0:
  41.4 28.7 all-gather.18
  72.3 47.3 all-gather.8
  121.8 46.8 all-gather.10
  170.8 46.8 all-gather.12
  219.2 49.1 all-gather.16
  270.6 32.2 all-gather.14
  341.9 56.5 all-reduce.1
  401.1 52.9 reduce-scatter.1
where the time goes:
time: 578 us; the launch traced here: 574 us
  waiting for transfers between devices  321 us (56%)
  blocking collectives  90.9 us (16%)
  matrix products  79.3 us (14%)
  local copies, waits for them, and re-layouts  24.9 us (4%)
  other arithmetic  21.6 us (4%)
  starting transfers between devices  20.8 us (4%)
  between operations  15.5 us (3%)
    pmax x1, blocking collectives, shards(): max_logit = lax.pmax(local_peaks, ('req', 'kv'))  68.5 us
    psum x1, waiting for transfers between devices, shards(): tail_sum = lax.psum(down_part[fresh_count - 1:], 'kv')  56 us
    reduce_scatter x1, waiting for transfers between devices, shards(): lax.psum_scatter(down_part, 'kv', scatter_dimension=0, tiled=True)  53.5 us
    all_gather x1, waiting for transfers between devices, shards(): o_full = lax.all_gather(o_proj, 'kv', axis=0, tiled=True)  49.7 us
    all_gather x1, waiting for transfers between devices, shards(): lax.all_gather(lax.dynamic_slice_in_dim(w_down, kv_index * ff_piece, ff_p...  48.9 us
    all_gather x1, waiting for transfers between devices, shards(): lax.all_gather(lax.dynamic_slice_in_dim(w_up, kv_index * ff_piece, ff_pie...  48.2 us
    all_gather x1, waiting for transfers between devices, shards(): lax.all_gather(pieces.reshape(tok_req, q_cols), 'kv', axis=1, tiled=True)  34.4 us
    all_gather x1, blocking collectives, shards(): lax.all_gather(tail_rows, 'req', axis=0, tiled=True)  22.4 us
  transfers between devices with their start and end apart: 10, of which 8 were waited for; matrix products, arithmetic and copies ran while one was open for 12% of the time, Pallas kernels for 0%

commit v1 on v0

--- a/solution.py
+++ b/solution.py
@@ -194,7 +194,11 @@
     going_back = jnp.zeros_like(out_rows).at[slot_place].set(out_rows)
     returned = regroup(going_back)
     layer_out = jnp.zeros_like(hidden_in).at[send_rows].set(returned)
-    tail_sum = lax.psum(down_part[fresh_count - 1 :], "kv")
+
+    def group_prepare(v0):
+        return lax.all_gather(v0, axis_name="kv").sum(axis=0)
+
+    tail_sum = group_prepare(down_part[fresh_count - 1 :])
     tail_out = (resid[fresh_count - 1 :].astype(jnp.float32) + tail_sum).astype(jnp.bfloat16)
     tail_rows = norm_rows(tail_out, final_gain).astype(jnp.bfloat16)
     local_peaks = jnp.max(

time: 578 us -> 516 us (0.89)
  waiting for transfers between devices: 321 us -> 245 us
  blocking collectives: 90.9 us -> 105 us
    psum x1 -> x0, waiting for transfers between devices: 56 us -> none  [shards(): tail_sum = lax.psum(down_part[fresh_count - 1:], 'kv')]
    reduce_scatter x1, waiting for transfers between devices: 53.5 us -> 35 us  [shards(): lax.psum_scatter(down_part, 'kv', scatter_dimension=0, tiled=True)]
    all_gather x0 -> x1, blocking collectives: none -> 14.4 us  [group_prepare(): return lax.all_gather(v0, axis_name='kv').sum(axis=0)]
  transfers between devices with their start and end apart: 10 -> 9, of which waited for: 8 -> 7; matrix products, arithmetic and copies ran while one was open for 12% -> 14% of each run, Pallas kernels for 0% -> 0%
where the time goes in v1:
time: 516 us; the launch traced here: 512 us
  waiting for transfers between devices  245 us (47%)
  blocking collectives  105 us (20%)
  matrix products  79.3 us (15%)
  local copies, waits for them, and re-layouts  24.2 us (5%)
  other arithmetic  21.6 us (4%)
  starting transfers between devices  20.7 us (4%)
  between operations  15.5 us (3%)
    pmax x1, blocking collectives, shards(): max_logit = lax.pmax(local_peaks, ('req', 'kv'))  68.4 us
    all_gather x1, waiting for transfers between devices, shards(): o_full = lax.all_gather(o_proj, 'kv', axis=0, tiled=True)  49.7 us
    all_gather x1, waiting for transfers between devices, shards(): lax.all_gather(lax.dynamic_slice_in_dim(w_down, kv_index * ff_piece, ff_p...  48.9 us
    all_gather x1, waiting for transfers between devices, shards(): lax.all_gather(lax.dynamic_slice_in_dim(w_up, kv_index * ff_piece, ff_pie...  48.2 us
    reduce_scatter x1, waiting for transfers between devices, shards(): lax.psum_scatter(down_part, 'kv', scatter_dimension=0, tiled=True)  35 us
    all_gather x1, waiting for transfers between devices, shards(): lax.all_gather(pieces.reshape(tok_req, q_cols), 'kv', axis=1, tiled=True)  34.4 us
    all_gather x1, blocking collectives, shards(): lax.all_gather(tail_rows, 'req', axis=0, tiled=True)  22.4 us
    all_to_all x2, starting transfers between devices, regroup(): lax.all_to_all(rows_in, ('req', 'kv'), split_axis=0, concat_axis=0, tiled...  19.9 us
  transfers between devices with their start and end apart: 9, of which 7 were waited for; matrix products, arithmetic and copies ran while one was open for 14% of the time, Pallas kernels for 0%

profile of v1, /device:TPU:1, one launch (start us, length us, event | category | flops | bytes accessed | tf_op | source)
XLA Modules:
  0.0 511.9 jit_solution(16865209602947537836)
XLA Ops:
  8.3 2.6 gather_fusion
  13.5 11.5 %all-to-all-start = ((bf16[128,2,1024]{2,1,0:T(2,128)(2,1)}), bf16[128,2,1024]{2,1,0:T(2,128)(2,1)S(1)}, u32[]{:S(2)}, u32[]{:S(2)}) async-start(bf16[128,2,1024]{2,1,0:T(2,128)(2,1)} %reshape.454), calls=%async_computation | async-start | bytes 1048576 | tf_op jit(solution)/shard_map/all_to_all | solution.py:77
  25.8 13.0 %all-to-all-done = bf16[128,2,1024]{2,1,0:T(2,128)(2,1)S(1)} async-done(((bf16[128,2,1024]{2,1,0:T(2,128)(2,1)}), bf16[128,2,1024]{2,1,0:T(2,128)(2,1)S(1)}, u32[]{:S(2)}, u32[]{:S(2)}) %all-to-all-start) | async-done | bytes 524320 | tf_op jit(solution)/shard_map/all_to_all | solution.py:77
  50.5 4.0 fusion.4
  54.5 15.6 %all-gather.21.cloned.1.call-done = bf16[1024,2048]{1,0:T(8,128)(2,1)} async-done(((bf16[128,2048]{1,0:T(8,128)(2,1)}), bf16[1024,2048]{1,0:T(8,128)(2,1)}) %all-gather.21.cloned.1.call-update) | async-done | bytes 4194320 | tf_op jit(solution)/shard_map/all_gather | solution.py:115
  70.1 3.2 fusion.10
  78.7 3.7 multiply_reduce_fusion.1
  88.2 3.6 convolution_convert_fusion
  92.6 15.9 %fusion.78 = (f32[2,1016]{1,0:T(2,128)S(1)}, f32[2,1016,3064]{2,1,0:T(8,128)}) fusion(pred[1016,3064]{1,0:T(8,128)(4,1)} %fusion.4, bf16[1016,128]{1,0:T(8,128)(2,1)S(1)} %copy.47, bf16[2048,128]{1,0:T(8,128)(2,1)S(1)} %bitcast.95, bf16[1024,2,64]{2,0,1:T(8,128)(2,1)S(1)} %get-tuple-element.10, bf16[1024,2,64]{2,0,1:T(8,128)(2,1)S(1)} %get-tuple-element.11), kind=kOutput, calls=%fused_computation.145 | convolution fusion | flops 1621384704 | bytes 29334016 | tf_op jit(solution)/shard_map/sub | solution.py:48
  108.5 12.0 %fusion.18 = bf16[1016,2,128]{2,0,1:T(8,128)(2,1)S(1)} fusion(f32[2,1016,3064]{2,1,0:T(8,128)} %get-tuple-element.25, f32[2,1016]{1,0:T(2,128)S(1)} %get-tuple-element.24, bf16[1016,128]{1,0:T(8,128)(2,1)S(1)} %slice.54, bf16[2048,128]{1,0:T(8,128)(2,1)S(1)} %bitcast.96), kind=kOutput, calls=%fused_computation.32 | convolution fusion | flops 1608149248 | bytes 26216896 | tf_op jit(solution)/shard_map/gck,kd->cgd/dot_general | solution.py:50
  120.5 48.2 %all-gather.13.cloned.1.call-done = bf16[2048,768]{0,1:T(8,128)(2,1)} async-done(((bf16[2048,48]{0,1:T(8,128)(2,1)}), bf16[2048,768]{0,1:T(8,128)(2,1)}) %all-gather.13.cloned.1.call-update) | async-done | bytes 3145744 | tf_op jit(solution)/shard_map/all_gather | solution.py:126
  168.8 48.9 %all-gather.15.cloned.1.call-done = bf16[768,2048]{1,0:T(8,128)(2,1)} async-done(((bf16[48,2048]{1,0:T(8,128)(2,1)}), bf16[768,2048]{1,0:T(8,128)(2,1)}) %all-gather.15.cloned.1.call-update) | async-done | bytes 3145744 | tf_op jit(solution)/shard_map/all_gather | solution.py:132
  218.8 49.7 %all-gather.19.cloned.1.call-done = bf16[2048,2048]{1,0:T(8,128)(2,1)} async-done(((bf16[256,2048]{1,0:T(8,128)(2,1)}), bf16[2048,2048]{1,0:T(8,128)(2,1)}) %all-gather.19.cloned.1.call-update) | async-done | bytes 8388624 | tf_op jit(solution)/shard_map/all_gather | solution.py:117
  268.5 34.4 %all-gather.17.cloned.1.call-done = bf16[1024,2048]{0,1:T(8,128)(2,1)} async-done(((bf16[1024,256]{0,1:T(8,128)(2,1)}), bf16[1024,2048]{0,1:T(8,128)(2,1)}) %all-gather.17.cloned.1.call-update) | async-done | bytes 4194320 | tf_op jit(solution)/shard_map/all_gather | solution.py:182
  302.9 14.2 %fusion.7 = (f32[1024]{0:T(1024)S(1)}, bf16[1024,2048]{1,0:T(8,128)(2,1)S(1)}) fusion(bf16[1024,2048]{0,1:T(8,128)(2,1)} %all-gather.17.cloned.1.call-done, bf16[2048,2048]{1,0:T(8,128)(2,1)} %all-gather.19.cloned.1.call-done, bf16[1024,2048]{1,0:T(8,128)(2,1)} %all-gather.21.cloned.1.call-done), kind=kOutput, calls=%fused_computation.20 | convolution fusion | flops 8602516480 | bytes 20975616 | tf_op jit(solution)/shard_map/dot_general | solution.py:184
  319.0 7.1 %fusion.20 = f32[1024,768]{1,0:T(8,128)} fusion(bf16[2048,768]{0,1:T(8,128)(2,1)} %all-gather.11.cloned.1.call-done, bf16[1024,2048]{1,0:T(8,128)(2,1)S(1)} %get-tuple-element.27, f32[2048]{0:T(1024)S(1)} %copy-done.17, f32[1024]{0:T(1024)S(1)} %add_rsqrt_fusion.1), kind=kOutput, calls=%fused_computation.33 | convolution fusion | flops 3229614080 | bytes 10498048 | tf_op jit(solution)/shard_map/dot_general | solution.py:187
  326.2 14.1 %fusion.23 = f32[1024,2048]{1,0:T(8,128)} fusion(bf16[768,2048]{1,0:T(8,128)(2,1)} %all-gather.15.cloned.1.call-done, f32[1024,768]{1,0:T(8,128)} %fusion.20, bf16[2048,768]{0,1:T(8,128)(2,1)} %all-gather.13.cloned.1.call-done, bf16[1024,2048]{1,0:T(8,128)(2,1)} %copy-done.7, f32[2048]{0:T(1024)S(1)} %copy-done.17, f32[1024]{0:T(1024)S(1)} %add_rsqrt_fusion.1), kind=kOutput, calls=%fused_computation.34 | convolution fusion | flops 6455558144 | bytes 22032384 | tf_op jit(solution)/shard_map/dot_general | solution.py:190
  341.2 14.4 %all-gather.2 = f32[8,9,2048]{2,1,0:T(8,128)S(1)} all-gather(f32[1,9,2048]{2,1,0:T(8,128)S(1)} %slice_bitcast_fusion), channel_id=3, replica_groups=mesh['req'=16,'kv'=8] {'kv'}, dimensions={0}, use_global_device_ids=true | all-gather | bytes 663552 | tf_op jit(solution)/shard_map/all_gather | solution.py:199
  357.6 35.0 %reduce-scatter.2.cloned.1.call-done = f32[128,2048]{1,0:T(8,128)} async-done(((f32[1024,2048]{1,0:T(8,128)}), f32[128,2048]{1,0:T(8,128)}) %reduce-scatter.2.cloned.1.call-update) | async-done | bytes 1048592 | tf_op jit(solution)/shard_map/reduce_scatter | solution.py:191
  392.5 2.6 scatter_custom_fusion
  397.3 8.4 %all-to-all-start.1 = ((bf16[128,2,1024]{2,1,0:T(2,128)(2,1)}), bf16[128,2,1024]{2,1,0:T(2,128)(2,1)S(1)}, u32[]{:S(2)}, u32[]{:S(2)}) async-start(bf16[128,2,1024]{2,1,0:T(2,128)(2,1)} %reshape.456), calls=%async_computation.2 | async-start | bytes 1048576 | tf_op jit(solution)/shard_map/all_to_all | solution.py:77
  405.7 22.4 %all-gather.3 = bf16[16,9,2048]{2,1,0:T(8,128)(2,1)S(1)} all-gather(bf16[1,9,2048]{2,1,0:T(8,128)(2,1)S(1)} %fusion.51), channel_id=1, replica_groups=mesh['req'=16,'kv'=8] {'req'}, dimensions={0}, use_global_device_ids=true | all-gather | bytes 626688 | tf_op jit(solution)/shard_map/all_gather | solution.py:206
  429.2 4.4 convolution_reduce_fusion
  433.6 68.4 %pmax.7 = f32[144]{0:T(256)} all-reduce(f32[144]{0:T(256)S(1)} %convolution_reduce_fusion), channel_id=1, replica_groups=mesh['req'=16,'kv'=8] {'req','kv'}, use_global_device_ids=true, to_apply=%region_15.16 | all-reduce | flops 144 | bytes 1152 | tf_op jit(solution)/shard_map/pmax | solution.py:212
  (113 shorter events, 39.3 us)
Async XLA Ops:
  7.2 34.2 %copy-start = (bf16[2048,384]{1,0:T(8,128)(2,1)S(1)}, bf16[2048,384]{1,0:T(8,128)(2,1)}, u32[]{:S(2)}) copy-start(bf16[2048,384]{1,0:T(8,128)(2,1)} %param.37) | copy-start | bytes 4718596
  13.5 25.2 %all-to-all-start = ((bf16[128,2,1024]{2,1,0:T(2,128)(2,1)}), bf16[128,2,1024]{2,1,0:T(2,128)(2,1)S(1)}, u32[]{:S(2)}, u32[]{:S(2)}) async-start(bf16[128,2,1024]{2,1,0:T(2,128)(2,1)} %reshape.454), calls=%async_computation | async-start | bytes 1048576 | tf_op jit(solution)/shard_map/all_to_all | solution.py:77
  25.0 45.1 %all-gather.21.cloned.1.call-start = ((), (), s32[]{:S(2)}) async-start(), calls=%async_computation.9 | async-start | bytes 4718592 | tf_op jit(solution)/shard_map/all_gather | solution.py:115
  41.2 7.2 %copy-start.10 = (s32[8]{0:T(128)S(1)}, s32[8]{0:T(128)}, u32[]{:S(2)}) copy-start(s32[8]{0:T(128)} %param.23) | copy-start | bytes 100
  41.3 79.3 %all-gather.11.cloned.1.call-start = ((), (), s32[]{:S(2)}) async-start(), calls=%async_computation.3 | async-start | bytes 3342336 | tf_op jit(solution)/shard_map/all_gather | solution.py:120
  42.5 126.3 %all-gather.13.cloned.1.call-start = ((), (), s32[]{:S(2)}) async-start(), calls=%async_computation.4 | async-start | bytes 3342336 | tf_op jit(solution)/shard_map/all_gather | solution.py:126
  44.9 172.8 %all-gather.15.cloned.1.call-start = ((), (), s32[]{:S(2)}) async-start(), calls=%async_computation.5 | async-start | bytes 3342336 | tf_op jit(solution)/shard_map/all_gather | solution.py:132
  46.6 221.9 %all-gather.19.cloned.1.call-start = ((), (), s32[]{:S(2)}) async-start(), calls=%async_computation.7 | async-start | bytes 9437184 | tf_op jit(solution)/shard_map/all_gather | solution.py:117
  47.2 255.7 %all-gather.17.cloned.1.call-start = ((), (), s32[]{:S(2)}) async-start(), calls=%async_computation.6 | async-start | bytes 4718592 | tf_op jit(solution)/shard_map/all_gather | solution.py:182
  48.5 24.9 %copy-start.8 = (f32[2048]{0:T(1024)S(1)}, f32[2048]{0:T(1024)}, u32[]{:S(2)}) copy-start(f32[2048]{0:T(1024)} %param.29) | copy-start | bytes 24580
  70.1 3.4 copy-start.2
  74.8 2.3 copy-start.3
  74.8 3.9 copy-start.6
  77.1 5.3 %copy-start.11 = (f32[128]{0:T(128)S(1)}, f32[128]{0:T(128)}, u32[]{:S(2)}) copy-start(f32[128]{0:T(128)} %param.34) | copy-start | bytes 1540
  78.7 5.4 %copy-start.12 = (f32[128]{0:T(128)S(1)}, f32[128]{0:T(128)}, u32[]{:S(2)}) copy-start(f32[128]{0:T(128)} %param.33) | copy-start | bytes 1540
  84.9 3.2 copy-start.14
  88.1 3.7 copy-start.5
  88.2 4.5 copy-start.15
  92.6 15.9 %copy-start.16 = (bf16[1,2048,128]{2,1,0:T(8,128)(2,1)S(1)}, bf16[1,2048,128]{2,1,0:T(8,128)(2,1)}, u32[]{:S(2)}) copy-start(bf16[1,2048,128]{2,1,0:T(8,128)(2,1)} %param.28) | copy-start | bytes 1572868
  218.7 100.3 %copy-start.17 = (f32[2048]{0:T(1024)S(1)}, f32[2048]{0:T(1024)}, u32[]{:S(2)}) copy-start(f32[2048]{0:T(1024)} %param.36) | copy-start | bytes 24580
  218.7 173.8 %reduce-scatter.2.cloned.1.call-start = ((), (), s32[]{:S(2)}) async-start(), calls=%async_computation.8 | async-start | bytes 9437184 | tf_op jit(solution)/shard_map/reduce_scatter | solution.py:191
  340.2 16.4 %copy-start.9 = (f32[2048]{0:T(1024)S(1)}, f32[2048]{0:T(1024)}, u32[]{:S(2)}) copy-start(f32[2048]{0:T(1024)} %param.40) | copy-start | bytes 24580
  397.3 104.7 %all-to-all-start.1 = ((bf16[128,2,1024]{2,1,0:T(2,128)(2,1)}), bf16[128,2,1024]{2,1,0:T(2,128)(2,1)S(1)}, u32[]{:S(2)}, u32[]{:S(2)}) async-start(bf16[128,2,1024]{2,1,0:T(2,128)(2,1)} %reshape.456), calls=%async_computation.2 | async-start | bytes 1048576 | tf_op jit(solution)/shard_map/all_to_all | solution.py:77
  428.1 76.7 %copy-start.1 = (bf16[2048,384]{1,0:T(8,128)(2,1)S(1)}, bf16[2048,384]{1,0:T(8,128)(2,1)}, u32[]{:S(2)}) copy-start(bf16[2048,384]{1,0:T(8,128)(2,1)} %param.37) | copy-start | bytes 4718596
  (3 other events, 5.4 us)
Sparse Core Ops, SparseCore 0:
  41.4 28.7 all-gather.20
  72.3 47.3 all-gather.10
  121.8 46.8 all-gather.12
  170.7 46.8 all-gather.14
  219.2 49.1 all-gather.18
  270.6 32.2 all-gather.16
  340.4 52.1 reduce-scatter.1
